TPU v7x, 512 devices: a whole 4x4x16 slice. The times are simulated.
512 devices in a mesh: prow: 16 (over x, y), pcol: 32 (over z, core).
Axes of the slice: x: 4, y: 4, z: 16, core: 2. Of those that a mesh axis runs over, the one named last changes fastest.
Arguments:
- adjoint_trail: float32 [2, 16, 256, 1, 32, 256], P(None, 'prow', None, None, 'pcol'), as said below
- factor_low: float32 [2, 16, 32, 8, 4, 256], P(None, 'prow', 'pcol'), may hold values from -0.0625 to 0.0625
- adjoint_low: float32 [2, 16, 32, 8, 4, 256], P(None, 'prow', 'pcol'), may hold values from -6 to 6
- factor_top: float32 [10, 256, 256], P(None, 'pcol'), as said below
- adjoint_top: float32 [10, 256, 256], P(None, 'pcol'), may hold values from -6 to 6
- diag_inverse: float32 [4, 256, 256], P(None, 'pcol'), as said below
Outputs:
- grad_low: float32 [2, 16, 32, 8, 4, 256], P(None, 'prow', 'pcol')
- grad_top: float32 [10, 256, 256], P(None, 'pcol')
Inputs may be any that keep to these rules, and one draw needn't show every extreme that they name: adjoint_trail reshaped row-major to 8192 x 8192 is symmetric. The diagonal blocks factor_top[j (j + 1) / 2 + j] are lower triangular with a positive diagonal. diag_inverse[j] is the inverse of factor_top[j (j + 1) / 2 + j].
All inputs are finite; a program needn't handle non-finite values.
Results may differ from a plain program's by a relative error of at most 0.00024.
Values sent between devices are 32-bit elements; how exact they have to be, the bound alone decides.
A program may use at most 64 MiB of HBM per device.

v0:
```python
import jax
import jax.numpy as jnp
from jax import lax
from jax.sharding import PartitionSpec as P

NB = 256
K = 4
HIGHEST = lax.Precision.HIGHEST


def from_root(array, axis, root):
    mine = lax.axis_index(axis) == root
    return lax.psum(jnp.where(mine, array, jnp.zeros_like(array)), axis)


def matmul(left, right):
    return jnp.dot(left, right, precision=HIGHEST, preferred_element_type=jnp.float32)


def inner_product(left, right):
    return lax.dot_general(
        left, right, (((0,), (0,)), ((), ())), precision=HIGHEST, preferred_element_type=jnp.float32
    )


def block_slot(row_block, col_block):
    return row_block * (row_block + 1) // 2 + col_block


def half_lower(square):
    size = square.shape[0]
    row_ids = lax.broadcasted_iota(jnp.int32, (size, size), 0)
    col_ids = lax.broadcasted_iota(jnp.int32, (size, size), 1)
    return jnp.where(row_ids > col_ids, square, jnp.where(row_ids == col_ids, 0.5 * square, 0.0))


def diagonal_adjoint(diagonal, inverse, lower_adj):
    inner = half_lower(inner_product(jnp.tril(diagonal), lower_adj))
    spread = inner_product(inverse, matmul(inner, inverse))
    return 0.5 * (spread + spread.T)


def rows_one(piece):
    return lax.all_gather(piece, "pcol", axis=1, tiled=True)


def owner_one(piece, root):
    return from_root(piece, "prow", root)


def reduce_one(term, count):
    return lax.psum_scatter(
        term(jnp.int32(0), lax.axis_size("pcol") * count), "pcol", scatter_dimension=0, tiled=True
    )


def trailing_product(trail, panels, gather_rows, send_owner, reduce_rows):
    prow_count = lax.axis_size("prow")
    pcol_count = lax.axis_size("pcol")
    cycles, sub_rows, width = panels.shape
    block = sub_rows * pcol_count
    gathered = gather_rows(panels[:, None]).reshape(cycles, block, width)
    column = lax.axis_index("pcol")
    col_cycles = trail.shape[3]
    global_block = 0 + column
    share = lax.dynamic_index_in_dim(gathered, global_block // prow_count, 0, keepdims=False)
    owned = [send_owner(share, global_block % prow_count)]
    stacked = jnp.stack(owned)
    view = trail.reshape(cycles, pcol_count, sub_rows, col_cycles, block)
    unit = cycles * sub_rows

    def term(start, count):
        product = jnp.einsum(
            "iaekb,kbn->aien", view, stacked, precision=HIGHEST, preferred_element_type=jnp.float32
        )
        return product.reshape(count, width)

    return reduce_rows(term, unit).reshape(cycles, sub_rows, width)


def per_device(adjoint_trail, factor_low, adjoint_low, factor_top, adjoint_top, diag_inverse):
    cycles = factor_low.shape[0]
    sub_rows = factor_low.shape[3]
    local_rows = cycles * sub_rows
    low_factor = factor_low.reshape(cycles, sub_rows, K * NB)
    low_adjoint = adjoint_low.reshape(local_rows, K, NB)
    columns = low_factor.reshape(local_rows, K, NB)
    top_factor, top_adjoint, inverses = (
        lax.all_gather(factor_top, "pcol", axis=1, tiled=True),
        lax.all_gather(adjoint_top, "pcol", axis=1, tiled=True),
        lax.all_gather(diag_inverse, "pcol", axis=1, tiled=True),
    )
    lower_grads = [None] * K
    diag_grads = [None] * K
    upper_grads = {}
    grams = {}

    def lower_step(panel):
        single = low_factor[:, :, panel * NB : (panel + 1) * NB]
        image = trailing_product(adjoint_trail, single, rows_one, owner_one, reduce_one).reshape(
            local_rows, NB
        )
        residual = low_adjoint[:, panel] - 2.0 * image
        for later in range(panel + 1, K):
            residual = residual - matmul(lower_grads[later], top_factor[block_slot(later, panel)])
        lower_grads[panel] = matmul(residual, inverses[panel])

    def top_step(panel):
        for row_block in range(panel + 1, K):
            top_residual = top_adjoint[block_slot(row_block, panel)] - grams[row_block, panel]
            top_residual = top_residual - 2.0 * matmul(
                diag_grads[row_block], top_factor[block_slot(row_block, panel)]
            )
            for middle in range(panel + 1, row_block):
                top_residual = top_residual - matmul(
                    upper_grads[middle, row_block], top_factor[block_slot(middle, panel)]
                )
            for beyond in range(row_block + 1, K):
                top_residual = top_residual - inner_product(
                    upper_grads[row_block, beyond], top_factor[block_slot(beyond, panel)]
                )
            upper_grads[panel, row_block] = matmul(top_residual, inverses[panel])
        lower_adj = top_adjoint[block_slot(panel, panel)] - grams[panel, panel]
        for row_block in range(panel + 1, K):
            lower_adj = lower_adj - inner_product(
                upper_grads[panel, row_block], top_factor[block_slot(row_block, panel)]
            )
        diag_grads[panel] = diagonal_adjoint(
            top_factor[block_slot(panel, panel)], inverses[panel], jnp.tril(lower_adj)
        )

    for panel in reversed(range(K)):
        lower_step(panel)
        local_gram = jnp.stack(
            [inner_product(lower_grads[panel], columns[:, earlier]) for earlier in range(panel + 1)]
        )
        summed = lax.psum(local_gram, ("prow", "pcol"))
        for earlier in range(panel + 1):
            grams[panel, earlier] = summed[earlier]
        top_step(panel)
    grad_low = jnp.stack(lower_grads, 1).reshape(factor_low.shape)
    blocks = []
    for row_block in range(K):
        for col_block in range(row_block + 1):
            if row_block == col_block:
                blocks.append(diag_grads[col_block])
            else:
                blocks.append(upper_grads[col_block, row_block])
    full_top = jnp.stack(blocks)
    share_rows = factor_top.shape[1]
    grad_top = lax.dynamic_slice_in_dim(
        full_top, lax.axis_index("pcol") * share_rows, share_rows, 1
    )
    return (grad_low, grad_top)


def solution(mesh):
    in_specs = (
        P(None, "prow", None, None, "pcol", None),
        P(None, "prow", "pcol", None, None, None),
        P(None, "prow", "pcol", None, None, None),
        P(None, "pcol", None),
        P(None, "pcol", None),
        P(None, "pcol", None),
    )
    out_specs = (P(None, "prow", "pcol", None, None, None), P(None, "pcol", None))
    return jax.shard_map(
        per_device, mesh=mesh, in_specs=in_specs, out_specs=out_specs, check_vma=False
    )
```

profile of v0, /device:TPU:8, one launch (start us, length us, event | category | flops | bytes accessed | tf_op | source)
XLA Modules:
  0.0 1294.8 jit_solution(6312719842912323253)
XLA Ops:
  9.0 37.8 %all-gather.3 = f32[2,256,256]{2,1,0:T(8,128)S(1)} all-gather(f32[2,8,256]{2,1,0:T(8,128)S(1)} %get-tuple-element.15), channel_id=5, replica_groups=mesh['prow'=16,'pcol'=32] {'pcol'}, dimensions={1}, use_global_device_ids=true | all-gather | bytes 540672 | tf_op jit(solution)/shard_map/all_gather | solution.py:44
  46.8 28.5 %all-gather.2 = f32[2,256,256]{2,1,0:T(8,128)S(1)} all-gather(f32[2,8,256]{2,1,0:T(8,128)S(1)} %get-tuple-element.16), channel_id=4, replica_groups=mesh['prow'=16,'pcol'=32] {'pcol'}, dimensions={1}, use_global_device_ids=true | all-gather | bytes 540672 | tf_op jit(solution)/shard_map/all_gather | solution.py:44
  76.7 29.8 %all-gather.1 = f32[2,256,256]{2,1,0:T(8,128)S(1)} all-gather(f32[2,8,256]{2,1,0:T(8,128)S(1)} %get-tuple-element.17), channel_id=3, replica_groups=mesh['prow'=16,'pcol'=32] {'pcol'}, dimensions={1}, use_global_device_ids=true | all-gather | bytes 540672 | tf_op jit(solution)/shard_map/all_gather | solution.py:44
  107.3 28.5 %all-gather = f32[2,256,256]{2,1,0:T(8,128)S(1)} all-gather(f32[2,8,256]{2,1,0:T(8,128)S(1)} %get-tuple-element.14), channel_id=2, replica_groups=mesh['prow'=16,'pcol'=32] {'pcol'}, dimensions={1}, use_global_device_ids=true | all-gather | bytes 540672 | tf_op jit(solution)/shard_map/all_gather | solution.py:44
  137.2 113.6 %all-reduce.7.cloned.1.call-done = (f32[256,256]{1,0:T(8,128)}, f32[256,256]{1,0:T(8,128)}, f32[256,256]{1,0:T(8,128)}, f32[256,256]{1,0:T(8,128)}) async-done(((f32[256,256]{1,0:T(8,128)}, f32[256,256]{1,0:T(8,128)}, f32[256,256]{1,0:T(8,128)}, f32[256,256]{1,0:T(8,128)}), (f32[256,256]{1,0:T(8,128)}, f32[256,256]{1,0:T(8,128)}, f32[256,256]{1,0:T(8,128)}, ...) | async-done | bytes 1048592 | tf_op jit(solution)/shard_map/psum | solution.py:13
  250.9 1.7 convolution_bitcast_fusion
  252.5 1.1 copy.31
  254.4 1.2 copy.29
  257.0 1.1 copy.27
  258.9 1.1 copy.25
  261.1 99.8 %reduce-scatter.11.cloned.1.call-done = f32[16,256]{1,0:T(8,128)} async-done(((f32[512,256]{1,0:T(8,128)}), f32[16,256]{1,0:T(8,128)}) %reduce-scatter.11.cloned.1.call-update) | async-done | bytes 16400 | tf_op jit(solution)/shard_map/reduce_scatter | solution.py:52
  360.9 1.2 fusion.67
  363.8 1.0 pad_maximum_fusion
  364.8 104.2 %reduce-scatter.9.cloned.1.call-done = f32[16,256]{1,0:T(8,128)} async-done(((f32[512,256]{1,0:T(8,128)}), f32[16,256]{1,0:T(8,128)}) %reduce-scatter.9.cloned.1.call-update) | async-done | bytes 16400 | tf_op jit(solution)/shard_map/reduce_scatter | solution.py:52
  469.0 72.4 %all-gather.10.cloned.1.call-done = f32[10,256,256]{2,1,0:T(8,128)} async-done(((f32[10,8,256]{2,1,0:T(8,128)}), f32[10,256,256]{2,1,0:T(8,128)}) %all-gather.10.cloned.1.call-update) | async-done | bytes 2621456 | tf_op jit(solution)/shard_map/all_gather | solution.py:89
  541.4 1.3 convolution_subtract_fusion.19
  542.8 1.1 fusion.70
  545.2 103.2 %reduce-scatter.7.cloned.1.call-done = f32[16,256]{1,0:T(8,128)} async-done(((f32[512,256]{1,0:T(8,128)}), f32[16,256]{1,0:T(8,128)}) %reduce-scatter.7.cloned.1.call-update) | async-done | bytes 16400 | tf_op jit(solution)/shard_map/reduce_scatter | solution.py:52
  648.4 1.2 convolution_subtract_fusion.18
  649.6 1.2 convolution_subtract_fusion.17
  650.8 1.1 fusion.74
  652.0 1.1 convolution_bitcast_fusion.11
  653.1 1.1 convolution_bitcast_fusion.12
  654.2 102.5 %reduce-scatter.5.cloned.1.call-done = f32[16,256]{1,0:T(8,128)} async-done(((f32[512,256]{1,0:T(8,128)}), f32[16,256]{1,0:T(8,128)}) %reduce-scatter.5.cloned.1.call-update) | async-done | bytes 16400 | tf_op jit(solution)/shard_map/reduce_scatter | solution.py:52
  758.2 1.2 fusion.79
  759.4 1.2 convolution_bitcast_fusion.13
  760.5 1.9 pad_maximum_fusion.2
  762.4 1.0 pad_maximum_fusion.1
  764.3 65.2 %all-gather.12.cloned.1.call-done = f32[10,256,256]{2,1,0:T(8,128)} async-done(((f32[10,8,256]{2,1,0:T(8,128)}), f32[10,256,256]{2,1,0:T(8,128)}) %all-gather.12.cloned.1.call-update) | async-done | bytes 2621456 | tf_op jit(solution)/shard_map/all_gather | solution.py:90
  829.5 417.1 %all-reduce.5.cloned.1.call-done = (f32[2,256,256]{2,1,0:T(8,128)}, f32[3,256,256]{2,1,0:T(8,128)}, f32[4,256,256]{2,1,0:T(8,128)}, f32[1,256,256]{2,1,0:T(8,128)}) async-done(((f32[2,256,256]{2,1,0:T(8,128)}, f32[3,256,256]{2,1,0:T(8,128)}, f32[4,256,256]{2,1,0:T(8,128)}, f32[1,256,256]{2,1,0:T(8,128)}), (f32[2,256,256]{2,1,0:T(8,128)}, f32[3,256,256]{2,1,0:T(8,128)}, f32[4,256,256]{2,1,0:T(8,128)}, ...) | async-done | bytes 2621456 | tf_op jit(solution)/shard_map/psum | solution.py:137
  1246.6 1.5 fusion.18
  1248.1 1.3 fusion.62
  1249.5 1.5 fusion.66
  1251.2 1.5 fusion.8
  1252.7 1.3 fusion.69
  1254.0 1.6 fusion.7
  1258.0 1.5 fusion.5
  1260.0 1.3 fusion.72
  1261.3 1.5 fusion.6
  1264.8 1.6 convolution_subtract_fusion.11
  1267.9 1.3 fusion.71
  1269.2 1.8 copy.38
  1271.0 1.5 fusion.1
  1272.5 1.5 fusion.2
  1276.7 1.4 fusion.3
  1279.8 1.6 convolution_subtract_fusion.6
  1284.4 1.0 bitcast_dynamic-update-slice_fusion.8
  1285.4 1.1 bitcast_dynamic-update-slice_fusion.7
  (138 shorter events, 27.5 us)
Async XLA Ops:
  8.0 242.9 %all-reduce.7.cloned.1.call-start = ((), (), s32[]{:S(2)}) async-start(), calls=%async_computation.12 | async-start | bytes 2097152 | tf_op jit(solution)/shard_map/psum | solution.py:13
  9.0 128.2 %copy-start.19 = (f32[2,1,256,1,1,256]{5,4,3,2,1,0:T(1,128)S(1)}, f32[2,1,256,1,1,256]{5,4,3,2,1,0:T(1,128)}, u32[]{:S(2)}) copy-start(f32[2,1,256,1,1,256]{5,4,3,2,1,0:T(1,128)} %param.6) | copy-start | bytes 1572868
  136.6 124.5 %all-gather.8.cloned.1.call-start = ((), (), s32[]{:S(2)}) async-start(), calls=%async_computation.8 | async-start | bytes 1081344 | tf_op jit(solution)/shard_map/all_gather | solution.py:91
  137.1 223.8 %reduce-scatter.11.cloned.1.call-start = ((), (), s32[]{:S(2)}) async-start(), calls=%async_computation.7 | async-start | bytes 540672 | tf_op jit(solution)/shard_map/reduce_scatter | solution.py:52
  250.8 2.9 copy-start.25
  250.9 5.5 copy-start.24
  253.7 215.4 %reduce-scatter.9.cloned.1.call-start = ((), (), s32[]{:S(2)}) async-start(), calls=%async_computation.6 | async-start | bytes 540672 | tf_op jit(solution)/shard_map/reduce_scatter | solution.py:52
  253.7 4.6 copy-start.23
  255.6 285.9 %all-gather.10.cloned.1.call-start = ((), (), s32[]{:S(2)}) async-start(), calls=%async_computation.9 | async-start | bytes 2703360 | tf_op jit(solution)/shard_map/all_gather | solution.py:89
  256.3 392.1 %reduce-scatter.7.cloned.1.call-start = ((), (), s32[]{:S(2)}) async-start(), calls=%async_computation.5 | async-start | bytes 540672 | tf_op jit(solution)/shard_map/reduce_scatter | solution.py:52
  256.4 4.6 copy-start.27
  257.0 3.9 copy-start.26
  258.2 498.6 %reduce-scatter.5.cloned.1.call-start = ((), (), s32[]{:S(2)}) async-start(), calls=%async_computation.4 | async-start | bytes 540672 | tf_op jit(solution)/shard_map/reduce_scatter | solution.py:52
  260.1 569.4 %all-gather.12.cloned.1.call-start = ((), (), s32[]{:S(2)}) async-start(), calls=%async_computation.10 | async-start | bytes 2703360 | tf_op jit(solution)/shard_map/all_gather | solution.py:90
  260.7 985.9 %all-reduce.5.cloned.1.call-start = ((), (), s32[]{:S(2)}) async-start(), calls=%async_computation.11 | async-start | bytes 5242880 | tf_op jit(solution)/shard_map/psum | solution.py:137
  541.4 215.3 %copy-start = (f32[10,256,256]{2,1,0:T(8,128)S(1)}, f32[10,256,256]{2,1,0:T(8,128)}, u32[]{:S(2)}) copy-start(f32[10,256,256]{2,1,0:T(8,128)} %all-gather.10.cloned.1.call-done) | copy-start | bytes 7864324
  1251.1 5.0 copy-start.1
  1258.0 3.3 copy-start.11
  1258.0 5.4 copy-start.2
  1259.6 5.2 copy-start.20
  1261.3 5.7 copy-start.7
  1264.1 0.7 copy-start.4
  1271.0 3.1 copy-start.8
  1271.0 3.9 copy-start.3
  1271.0 4.3 copy-start.5
  1274.4 2.2 copy-start.10
  1274.4 2.2 copy-start.16
  1274.4 2.2 copy-start.21
  1275.2 6.8 copy-start.14
  1276.2 3.5 copy-start.22
  1276.7 4.7 copy-start.17
  1279.7 3.9 copy-start.13
  1283.2 3.3 copy-start.18
  1283.2 3.3 copy-start.6
  1283.2 3.3 copy-start.12
  1283.6 3.0 copy-start.15
  1284.2 2.4 copy-start.9
Sparse Core Ops, SparseCore 0:
  136.7 114.1 all-reduce.6
  763.6 482.9 all-reduce.4
Sparse Core Ops, SparseCore 1:
  139.2 67.6 all-gather.7
  253.7 107.1 reduce-scatter.10
  363.8 105.2 reduce-scatter.8
  471.2 70.2 all-gather.9
  544.2 104.1 reduce-scatter.6
  651.4 105.3 reduce-scatter.4
  758.8 70.6 all-gather.11
where the time goes:
time: 1300 us; the launch traced here: 1290 us
  waiting for transfers between devices  1080 us (83%)
  blocking collectives  125 us (10%)
  matrix products  53.2 us (4%)
  between operations  16.7 us (1%)
    psum x1, waiting for transfers between devices, per_device(): summed = lax.psum(local_gram, ('prow', 'pcol'))  417 us
    reduce_scatter x4, waiting for transfers between devices, reduce_one(): lax.psum_scatter(term(jnp.int32(0), lax.axis_size('pcol') * count), 'pcol...  410 us
    all_gather x4, blocking collectives, rows_one(): return lax.all_gather(piece, 'pcol', axis=1, tiled=True)  125 us
    psum x1, waiting for transfers between devices, from_root(): return lax.psum(jnp.where(mine, array, jnp.zeros_like(array)), axis)  114 us
    all_gather x1, waiting for transfers between devices, per_device(): lax.all_gather(factor_top, 'pcol', axis=1, tiled=True)  72.4 us
    all_gather x1, waiting for transfers between devices, per_device(): lax.all_gather(adjoint_top, 'pcol', axis=1, tiled=True)  65.2 us
    dot_general x30, matrix products, matmul(): jnp.dot(left, right, precision=HIGHEST, preferred_element_type=jnp.float32)  27.1 us
  transfers between devices with their start and end apart: 9, of which 8 were waited for; matrix products, arithmetic and copies ran while one was open for 2% of the time, Pallas kernels for 0%

commit v1 on v0

--- a/solution.py
+++ b/solution.py
@@ -2,6 +2,7 @@
 import jax.numpy as jnp
 from jax import lax
 from jax.sharding import PartitionSpec as P
+from jax.lax import psum
 
 NB = 256
 K = 4
@@ -134,7 +135,9 @@
         local_gram = jnp.stack(
             [inner_product(lower_grads[panel], columns[:, earlier]) for earlier in range(panel + 1)]
         )
-        summed = lax.psum(local_gram, ("prow", "pcol"))
+        summed = local_gram
+        for j in ("pcol", "prow"):
+            summed = psum(summed, axis_name=j)
         for earlier in range(panel + 1):
             grams[panel, earlier] = summed[earlier]
         top_step(panel)

time: 1300 us -> 1150 us (0.88)
  the two profiles are of different devices: /device:TPU:8 before, /device:TPU:1 now
where the time goes in v1:
time: 1150 us
  waiting for transfers between devices  934 us (81%)
  blocking collectives  126 us (11%)
  matrix products  53.2 us (5%)
  between operations  16.7 us (1%)
    reduce_scatter x4, waiting for transfers between devices, reduce_one(): lax.psum_scatter(term(jnp.int32(0), lax.axis_size('pcol') * count), 'pcol...  405 us
    psum x2, waiting for transfers between devices, per_device(): summed = psum(summed, axis_name=j)  264 us
    all_gather x4, blocking collectives, rows_one(): return lax.all_gather(piece, 'pcol', axis=1, tiled=True)  126 us
    psum x1, waiting for transfers between devices, from_root(): return lax.psum(jnp.where(mine, array, jnp.zeros_like(array)), axis)  112 us
    all_gather x1, waiting for transfers between devices, per_device(): lax.all_gather(factor_top, 'pcol', axis=1, tiled=True)  76.1 us
    all_gather x1, waiting for transfers between devices, per_device(): lax.all_gather(adjoint_top, 'pcol', axis=1, tiled=True)  74.6 us
    dot_general x30, matrix products, matmul(): jnp.dot(left, right, precision=HIGHEST, preferred_element_type=jnp.float32)  27.1 us
  transfers between devices with their start and end apart: 10, of which 9 were waited for; matrix products, arithmetic and copies ran while one was open for 2% of the time, Pallas kernels for 0%

profile of v1, /device:TPU:1, one launch (start us, length us, event | category | flops | bytes accessed | tf_op | source)
XLA Modules:
  0.0 1150.1 jit_solution(15074182320154749252)
XLA Ops:
  9.0 39.1 %all-gather.3 = f32[2,256,256]{2,1,0:T(8,128)S(1)} all-gather(f32[2,8,256]{2,1,0:T(8,128)S(1)} %get-tuple-element.19), channel_id=5, replica_groups=mesh['prow'=16,'pcol'=32] {'pcol'}, dimensions={1}, use_global_device_ids=true | all-gather | bytes 540672 | tf_op jit(solution)/shard_map/all_gather | solution.py:45
  48.1 28.5 %all-gather.2 = f32[2,256,256]{2,1,0:T(8,128)S(1)} all-gather(f32[2,8,256]{2,1,0:T(8,128)S(1)} %get-tuple-element.20), channel_id=4, replica_groups=mesh['prow'=16,'pcol'=32] {'pcol'}, dimensions={1}, use_global_device_ids=true | all-gather | bytes 540672 | tf_op jit(solution)/shard_map/all_gather | solution.py:45
  78.1 29.8 %all-gather.1 = f32[2,256,256]{2,1,0:T(8,128)S(1)} all-gather(f32[2,8,256]{2,1,0:T(8,128)S(1)} %get-tuple-element.21), channel_id=3, replica_groups=mesh['prow'=16,'pcol'=32] {'pcol'}, dimensions={1}, use_global_device_ids=true | all-gather | bytes 540672 | tf_op jit(solution)/shard_map/all_gather | solution.py:45
  108.6 28.5 %all-gather = f32[2,256,256]{2,1,0:T(8,128)S(1)} all-gather(f32[2,8,256]{2,1,0:T(8,128)S(1)} %get-tuple-element.18), channel_id=2, replica_groups=mesh['prow'=16,'pcol'=32] {'pcol'}, dimensions={1}, use_global_device_ids=true | all-gather | bytes 540672 | tf_op jit(solution)/shard_map/all_gather | solution.py:45
  138.5 112.3 %all-reduce.11.cloned.1.call-done = (f32[256,256]{1,0:T(8,128)}, f32[256,256]{1,0:T(8,128)}, f32[256,256]{1,0:T(8,128)}, f32[256,256]{1,0:T(8,128)}) async-done(((f32[256,256]{1,0:T(8,128)}, f32[256,256]{1,0:T(8,128)}, f32[256,256]{1,0:T(8,128)}, f32[256,256]{1,0:T(8,128)}), (f32[256,256]{1,0:T(8,128)}, f32[256,256]{1,0:T(8,128)}, f32[256,256]{1,0:T(8,128)}, ...) | async-done | bytes 1048592 | tf_op jit(solution)/shard_map/psum | solution.py:14
  250.8 1.7 convolution_bitcast_fusion
  252.5 1.1 copy.31
  254.4 1.1 copy.29
  257.0 1.1 copy.27
  259.0 1.1 copy.25
  260.2 98.6 %reduce-scatter.11.cloned.1.call-done = f32[16,256]{1,0:T(8,128)} async-done(((f32[512,256]{1,0:T(8,128)}), f32[16,256]{1,0:T(8,128)}) %reduce-scatter.11.cloned.1.call-update) | async-done | bytes 16400 | tf_op jit(solution)/shard_map/reduce_scatter | solution.py:53
  358.8 1.2 fusion.67
  361.7 1.0 pad_maximum_fusion
  362.7 104.0 %reduce-scatter.9.cloned.1.call-done = f32[16,256]{1,0:T(8,128)} async-done(((f32[512,256]{1,0:T(8,128)}), f32[16,256]{1,0:T(8,128)}) %reduce-scatter.9.cloned.1.call-update) | async-done | bytes 16400 | tf_op jit(solution)/shard_map/reduce_scatter | solution.py:53
  466.7 76.1 %all-gather.10.cloned.1.call-done = f32[10,256,256]{2,1,0:T(8,128)} async-done(((f32[10,8,256]{2,1,0:T(8,128)}), f32[10,256,256]{2,1,0:T(8,128)}) %all-gather.10.cloned.1.call-update) | async-done | bytes 2621456 | tf_op jit(solution)/shard_map/all_gather | solution.py:90
  542.7 1.3 convolution_subtract_fusion.19
  544.1 1.1 fusion.70
  546.5 100.2 %reduce-scatter.7.cloned.1.call-done = f32[16,256]{1,0:T(8,128)} async-done(((f32[512,256]{1,0:T(8,128)}), f32[16,256]{1,0:T(8,128)}) %reduce-scatter.7.cloned.1.call-update) | async-done | bytes 16400 | tf_op jit(solution)/shard_map/reduce_scatter | solution.py:53
  646.7 1.2 convolution_subtract_fusion.18
  647.9 1.2 convolution_subtract_fusion.17
  649.1 1.1 fusion.74
  650.2 1.1 convolution_bitcast_fusion.11
  651.4 1.1 convolution_bitcast_fusion.12
  652.5 102.3 %reduce-scatter.5.cloned.1.call-done = f32[16,256]{1,0:T(8,128)} async-done(((f32[512,256]{1,0:T(8,128)}), f32[16,256]{1,0:T(8,128)}) %reduce-scatter.5.cloned.1.call-update) | async-done | bytes 16400 | tf_op jit(solution)/shard_map/reduce_scatter | solution.py:53
  756.2 1.2 fusion.79
  757.4 1.1 convolution_bitcast_fusion.13
  758.6 1.9 pad_maximum_fusion.2
  762.3 216.0 %all-reduce.7.cloned.1.call-done = (f32[2,256,256]{2,1,0:T(8,128)}, f32[3,256,256]{2,1,0:T(8,128)}, f32[4,256,256]{2,1,0:T(8,128)}, f32[1,256,256]{2,1,0:T(8,128)}) async-done(((f32[2,256,256]{2,1,0:T(8,128)}, f32[3,256,256]{2,1,0:T(8,128)}, f32[4,256,256]{2,1,0:T(8,128)}, f32[1,256,256]{2,1,0:T(8,128)}), (f32[2,256,256]{2,1,0:T(8,128)}, f32[3,256,256]{2,1,0:T(8,128)}, f32[4,256,256]{2,1,0:T(8,128)}, ...) | async-done | bytes 2621456 | tf_op jit(solution)/shard_map/psum | solution.py:140
  979.1 74.6 %all-gather.12.cloned.1.call-done = f32[10,256,256]{2,1,0:T(8,128)} async-done(((f32[10,8,256]{2,1,0:T(8,128)}), f32[10,256,256]{2,1,0:T(8,128)}) %all-gather.12.cloned.1.call-update) | async-done | bytes 2621456 | tf_op jit(solution)/shard_map/all_gather | solution.py:91
  1053.6 48.2 %all-reduce.9.cloned.1.call-done = (f32[2,256,256]{2,1,0:T(8,128)}, f32[3,256,256]{2,1,0:T(8,128)}, f32[4,256,256]{2,1,0:T(8,128)}, f32[1,256,256]{2,1,0:T(8,128)}) async-done(((f32[2,256,256]{2,1,0:T(8,128)}, f32[3,256,256]{2,1,0:T(8,128)}, f32[4,256,256]{2,1,0:T(8,128)}, f32[1,256,256]{2,1,0:T(8,128)}), (f32[2,256,256]{2,1,0:T(8,128)}, f32[3,256,256]{2,1,0:T(8,128)}, f32[4,256,256]{2,1,0:T(8,128)}, ...) | async-done | bytes 2621456 | tf_op jit(solution)/shard_map/psum | solution.py:140
  1101.8 1.5 fusion.18
  1103.4 1.3 fusion.62
  1104.7 1.5 fusion.66
  1106.5 1.5 fusion.8
  1108.0 1.3 fusion.69
  1109.3 1.6 fusion.7
  1113.3 1.5 fusion.5
  1115.2 1.3 fusion.72
  1116.6 1.5 fusion.6
  1119.9 1.6 convolution_subtract_fusion.11
  1123.0 1.3 fusion.71
  1124.3 1.8 copy.38
  1126.1 1.5 fusion.1
  1127.6 1.5 fusion.2
  1132.0 1.4 fusion.3
  1135.1 1.6 convolution_subtract_fusion.6
  1139.8 1.0 bitcast_dynamic-update-slice_fusion.8
  1140.7 1.1 bitcast_dynamic-update-slice_fusion.7
  (141 shorter events, 28.5 us)
Async XLA Ops:
  8.0 242.8 %all-reduce.11.cloned.1.call-start = ((), (), s32[]{:S(2)}) async-start(), calls=%async_computation.13 | async-start | bytes 2097152 | tf_op jit(solution)/shard_map/psum | solution.py:14
  9.0 129.5 %copy-start.19 = (f32[2,1,256,1,1,256]{5,4,3,2,1,0:T(1,128)S(1)}, f32[2,1,256,1,1,256]{5,4,3,2,1,0:T(1,128)}, u32[]{:S(2)}) copy-start(f32[2,1,256,1,1,256]{5,4,3,2,1,0:T(1,128)} %param.6) | copy-start | bytes 1572868
  137.9 122.3 %all-gather.8.cloned.1.call-start = ((), (), s32[]{:S(2)}) async-start(), calls=%async_computation.8 | async-start | bytes 1081344 | tf_op jit(solution)/shard_map/all_gather | solution.py:92
  138.4 220.4 %reduce-scatter.11.cloned.1.call-start = ((), (), s32[]{:S(2)}) async-start(), calls=%async_computation.7 | async-start | bytes 540672 | tf_op jit(solution)/shard_map/reduce_scatter | solution.py:53
  250.8 2.8 copy-start.25
  250.8 5.5 copy-start.24
  253.6 213.1 %reduce-scatter.9.cloned.1.call-start = ((), (), s32[]{:S(2)}) async-start(), calls=%async_computation.6 | async-start | bytes 540672 | tf_op jit(solution)/shard_map/reduce_scatter | solution.py:53
  253.7 4.5 copy-start.27
  254.3 3.9 copy-start.26
  254.4 3.9 copy-start.23
  255.5 287.2 %all-gather.10.cloned.1.call-start = ((), (), s32[]{:S(2)}) async-start(), calls=%async_computation.9 | async-start | bytes 2703360 | tf_op jit(solution)/shard_map/all_gather | solution.py:90
  256.3 390.4 %reduce-scatter.7.cloned.1.call-start = ((), (), s32[]{:S(2)}) async-start(), calls=%async_computation.5 | async-start | bytes 540672 | tf_op jit(solution)/shard_map/reduce_scatter | solution.py:53
  258.1 496.7 %reduce-scatter.5.cloned.1.call-start = ((), (), s32[]{:S(2)}) async-start(), calls=%async_computation.4 | async-start | bytes 540672 | tf_op jit(solution)/shard_map/reduce_scatter | solution.py:53
  260.1 718.2 %all-reduce.7.cloned.1.call-start = ((), (), s32[]{:S(2)}) async-start(), calls=%async_computation.11 | async-start | bytes 5242880 | tf_op jit(solution)/shard_map/psum | solution.py:140
  542.7 212.1 %copy-start = (f32[10,256,256]{2,1,0:T(8,128)S(1)}, f32[10,256,256]{2,1,0:T(8,128)}, u32[]{:S(2)}) copy-start(f32[10,256,256]{2,1,0:T(8,128)} %all-gather.10.cloned.1.call-done) | copy-start | bytes 7864324
  761.4 292.2 %all-gather.12.cloned.1.call-start = ((), (), s32[]{:S(2)}) async-start(), calls=%async_computation.10 | async-start | bytes 2703360 | tf_op jit(solution)/shard_map/all_gather | solution.py:91
  762.0 339.8 %all-reduce.9.cloned.1.call-start = ((), (), s32[]{:S(2)}) async-start(), calls=%async_computation.12 | async-start | bytes 5242880 | tf_op jit(solution)/shard_map/psum | solution.py:140
  1106.4 5.0 copy-start.1
  1113.3 3.3 copy-start.11
  1113.3 5.4 copy-start.2
  1114.8 5.0 copy-start.20
  1116.6 5.5 copy-start.7
  1119.1 0.7 copy-start.4
  1126.1 3.1 copy-start.8
  1126.1 3.9 copy-start.3
  1126.1 4.3 copy-start.5
  1129.5 2.4 copy-start.10
  1129.6 2.4 copy-start.16
  1129.6 2.4 copy-start.21
  1130.4 7.0 copy-start.14
  1131.6 3.5 copy-start.22
  1132.0 4.7 copy-start.17
  1135.1 3.9 copy-start.13
  1138.5 3.3 copy-start.18
  1138.5 3.3 copy-start.6
  1138.5 3.3 copy-start.12
  1139.0 3.0 copy-start.15
  1139.6 2.4 copy-start.9
Sparse Core Ops, SparseCore 0:
  138.0 112.7 all-reduce.10
  978.4 123.4 all-reduce.8
Sparse Core Ops, SparseCore 1:
  140.5 67.5 all-gather.7
  253.7 105.0 reduce-scatter.10
  361.7 104.9 reduce-scatter.8
  468.8 73.8 all-gather.9
  545.5 101.1 reduce-scatter.6
  649.7 105.1 reduce-scatter.4
  761.5 216.7 all-reduce.6
  980.5 73.1 all-gather.11
